TPU v7x, 32 devices: a whole 2x2x4 slice. The times are simulated.
32 devices in a mesh: groups: 1, row: 32 (over z, y, x, core).
Axes of the slice: x: 2, y: 2, z: 4, core: 2. Of those that a mesh axis runs over, the one named last changes fastest.
Arguments:
- pair_mantissa: bfloat16 [128, 128, 128], P(('groups', 'row')), may hold values from -6 to 6
- pair_exponent: int32 [128, 1, 128], P(('groups', 'row')), may hold values from -3 to 3
- residue_mask: int32 [128], P('groups'), may hold values 0 or 1
- ln_gain: float32 [128], replicated, may hold values from 0.25 to 1.75
- ln_shift: float32 [128], replicated, may hold values from -3 to 3
- w_proj: bfloat16 [128, 512], replicated, may hold values from -10 to 10
- w_bias: bfloat16 [128, 4], replicated, may hold values from -0.5 to 0.5
- gate_shift: float32 [128], replicated, may hold values from -4 to 4
- w_out: bfloat16 [128, 128], replicated, may hold values from -0.5 to 0.5
- out_shift: float32 [128], replicated, may hold values from -3 to 3
Outputs:
- update: bfloat16 [32, 128, 128], P(('groups', 'row'))
All inputs are finite; a program needn't handle non-finite values.
Results may differ from a plain program's by a relative error of at most 0.005.
Values may be sent and summed in bfloat16 or wider, within the bound.
A program may use at most 64 MiB of HBM per device.

v0:
```python
import jax
import jax.numpy as jnp
from jax import lax
from jax.sharding import PartitionSpec as P

WD = 1
epsilon = 1e-05
big_negative = 1000000000.0


def dequantize(mantissa, exponent):
    scaling = jnp.zeros(exponent.shape, jnp.float32)
    for expo_level in range(-3, 4):
        scaling = scaling + jnp.where(
            exponent == expo_level, jnp.float32(2.0**expo_level), jnp.float32(0.0)
        )
    row_count, block_count, channels = exponent.shape
    block_width = mantissa.shape[1] // block_count
    scaling = jnp.broadcast_to(
        scaling[:, :, None, :], (row_count, block_count, block_width, channels)
    )
    return mantissa.astype(jnp.float32) * scaling.reshape(
        row_count, block_count * block_width, channels
    )


def normalize(mantissa, exponent, ln_gain, ln_shift):
    values = dequantize(mantissa, exponent)
    center = jnp.mean(values, axis=-1, keepdims=True)
    spread = jnp.mean(jnp.square(values - center), axis=-1, keepdims=True)
    return ((values - center) * lax.rsqrt(spread + epsilon) * ln_gain + ln_shift).astype(
        jnp.bfloat16
    )


def project(columns, w_proj, gate_shift, inner_width, window_rows, head_size):
    key_value = jnp.einsum(
        "lmc,cd->mld",
        columns,
        w_proj[:, inner_width : 3 * inner_width],
        preferred_element_type=jnp.float32,
    ).astype(jnp.bfloat16)
    query_weight = jnp.concatenate([w_proj[:, :inner_width], w_proj[:, 3 * inner_width :]], axis=1)
    query_gate = jnp.einsum(
        "wmc,cd->mwd", columns[:window_rows], query_weight, preferred_element_type=jnp.float32
    )
    queries = (query_gate[..., :inner_width] * head_size ** (-0.5)).astype(jnp.bfloat16)
    gating = jax.nn.sigmoid(query_gate[..., inner_width:] + gate_shift)
    return (key_value, queries, gating)


def finish(gating, attended, w_out, out_shift):
    gated_out = (gating * attended).astype(jnp.bfloat16)
    return (
        jnp.einsum("mwd,dc->mwc", gated_out, w_out, preferred_element_type=jnp.float32) + out_shift
    ).astype(jnp.bfloat16)


def attend_whole(columns, key_bias, mask_bias, w_proj, gate_shift, w_out, out_shift):
    inner_width = w_out.shape[0]
    head_count = key_bias.shape[1]
    head_size = inner_width // head_count
    window_rows = key_bias.shape[2]
    key_value, queries, gating = project(
        columns, w_proj, gate_shift, inner_width, window_rows, head_size
    )

    def single_column(operands):
        kv_column, query_column = operands
        key_heads = kv_column[:, :inner_width].reshape(-1, head_count, head_size)
        value_heads = kv_column[:, inner_width:].reshape(-1, head_count, head_size)
        query_heads = query_column.reshape(window_rows, head_count, head_size)
        scores = jnp.einsum(
            "lhd,whd->lhw", key_heads, query_heads, preferred_element_type=jnp.float32
        )
        scores = scores + key_bias.astype(jnp.float32) + mask_bias[:, None, None]
        row_max = jnp.max(scores, axis=0)
        weights = jnp.exp(scores - row_max)
        denominator = jnp.sum(weights, axis=0)
        attended = jnp.einsum(
            "lhw,lhd->whd",
            weights.astype(jnp.bfloat16),
            value_heads,
            preferred_element_type=jnp.float32,
        )
        return (attended / denominator.T[:, :, None]).reshape(window_rows, inner_width)

    attended = lax.map(single_column, (key_value, queries))
    return finish(gating, attended, w_out, out_shift)


def per_device(
    pair_mantissa,
    pair_exponent,
    residue_mask,
    ln_gain,
    ln_shift,
    w_proj,
    w_bias,
    gate_shift,
    w_out,
    out_shift,
):
    devices_row = lax.axis_size("row")
    local_rows = pair_mantissa.shape[0]
    channels = pair_mantissa.shape[2]
    window_rows = WD * devices_row
    normal = normalize(pair_mantissa, pair_exponent, ln_gain, ln_shift)
    local_bias = jnp.einsum(
        "rwc,ch->rhw", normal[:, :window_rows], w_bias, preferred_element_type=jnp.float32
    ).astype(jnp.bfloat16)
    mask_bias = big_negative * (residue_mask.astype(jnp.float32) - 1.0)
    split_pair = normal.reshape(local_rows, devices_row, local_rows, channels)
    key_bias = lax.all_gather(local_bias, "row", axis=0, tiled=True)
    received = lax.all_to_all(split_pair, "row", split_axis=1, concat_axis=0, tiled=True)
    result = attend_whole(received[:, 0], key_bias, mask_bias, w_proj, gate_shift, w_out, out_shift)
    row_layout = lax.all_to_all(result, "row", split_axis=1, concat_axis=0, tiled=True)
    return jnp.transpose(row_layout, (1, 0, 2))


def solution(mesh):
    in_specs = (
        P(("groups", "row"), None, None),
        P(("groups", "row"), None, None),
        P("groups"),
        P(),
        P(),
        P(),
        P(),
        P(),
        P(),
        P(),
    )
    out_specs = P(("groups", "row"), None, None)
    return jax.shard_map(
        per_device, mesh=mesh, in_specs=in_specs, out_specs=out_specs, check_vma=False
    )
```

profile of v0, /device:TPU:0, one launch (start us, length us, event | category | flops | bytes accessed | tf_op | source)
XLA Modules:
  0.0 68.8 jit_solution(6774469167850363746)
XLA Ops:
  0.0 0.0 copy-start
  0.0 0.0 copy-start.1
  0.0 0.7 %fusion.32 = f32[4,1,128]{2,1,0:T(1,128)S(1)} fusion(s32[4,1,128]{2,1,0:T(1,128)} %param.13), kind=kLoop, calls=%fused_computation.53 | loop fusion | flops 10240 | bytes 4096 | tf_op jit(solution)/shard_map/add | solution.py:14
  0.7 1.1 %fusion.12 = f32[4,128]{1,0:T(4,128)S(1)} fusion(bf16[4,128,128]{2,1,0:T(8,128)(2,1)} %param.12, f32[4,128]{1,0:T(4,128)S(1)} %bitcast.76), kind=kLoop, calls=%fused_computation.24 | loop fusion | flops 196096 | bytes 135168 | tf_op jit(solution)/shard_map/reduce_sum | solution.py:29
  1.8 0.0 copy-done.1
  1.8 0.2 multiply_reduce_fusion
  2.1 0.0 copy-start.3
  2.1 0.0 copy-start.4
  2.1 0.6 copy-done.3
  2.7 0.0 copy-done.4
  2.7 0.2 add_convert_fusion
  2.9 0.7 %copy.18 = bf16[4,32,4,128]{3,0,2,1:T(4,128)(2,1)} copy(bf16[4,32,4,128]{3,2,1,0:T(4,128)(2,1)S(1)} %bitcast.72) | data formatting | bytes 262144 | tf_op jit(solution)/shard_map/reshape | solution.py:113
  3.7 0.0 copy-start.5
  3.7 7.3 %all-to-all-start = ((bf16[4,32,4,128]{3,0,2,1:T(4,128)(2,1)}), bf16[4,32,4,128]{3,0,2,1:T(4,128)(2,1)S(1)}, u32[]{:S(2)}, u32[]{:S(2)}) async-start(bf16[4,32,4,128]{3,0,2,1:T(4,128)(2,1)} %copy.18), calls=%async_computation | async-start | bytes 262144 | tf_op jit(solution)/shard_map/all_to_all | solution.py:115
  11.0 0.0 copy-done.5
  11.0 0.0 copy-start.6
  11.1 0.1 fusion.10
  11.2 0.5 copy-done.6
  11.7 0.0 copy-start.2
  11.7 42.2 %all_gather.3 = bf16[128,4,32]{2,1,0:T(4,128)(2,1)S(1)} all-gather(bf16[4,4,32]{2,1,0:T(4,128)(2,1)S(1)} %fusion.10), channel_id=1, replica_groups=mesh['groups'=1,'row'=32] {'row'}, dimensions={0}, use_global_device_ids=true | all-gather | bytes 33792 | tf_op jit(solution)/shard_map/all_gather | solution.py:114
  53.9 0.1 copy.22
  54.0 0.0 copy-done.2
  54.1 0.0 all-to-all-done
  54.2 0.2 convolution_bitcast_fusion.2
  54.3 0.2 fusion.8
  54.6 3.8 %while.10 = (s32[]{:T(128)}, f32[4,32,128]{2,1,0:T(8,128)S(1)}, bf16[4,128,256]{2,1,0:T(8,128)(2,1)S(1)}, bf16[4,32,128]{2,1,0:T(8,128)(2,1)S(1)}, bf16[128,4,32...) while((s32[]{:T(128)}, f32[4,32,128]{2,1,0:T(8,128)S(1)}, bf16[4,128,256]{2,1,0:T(8,128)(2,1)S(1)}, ...), condition=%wide.region_5.6_spmd, body=%wide.region_2.5_spmd.sunk | while | flops 2232066 | bytes 814169 | solution.py:88
  54.6 0.1 copy.38
  54.7 0.1 reshape.53
  54.8 0.2 fusion.54
  55.0 0.2 fusion.55
  55.2 0.2 fusion.56
  55.4 0.1 copy.39
  55.5 0.1 copy.38
  55.7 0.1 reshape.53
  55.8 0.2 fusion.54
  56.0 0.2 fusion.55
  56.2 0.2 fusion.56
  56.4 0.1 copy.39
  56.5 0.1 copy.38
  56.6 0.1 reshape.53
  56.7 0.2 fusion.54
  56.9 0.2 fusion.55
  57.1 0.2 fusion.56
  57.3 0.1 copy.39
  57.4 0.1 copy.38
  57.6 0.1 reshape.53
  57.7 0.2 fusion.54
  57.9 0.2 fusion.55
  58.1 0.2 fusion.56
  58.3 0.1 copy.39
  58.3 0.0 copy-start.7
  58.4 0.0 copy-start.8
  58.4 0.0 copy-done
  58.4 0.6 copy-done.7
  59.0 0.0 copy-done.8
  59.0 0.1 fusion.9
  59.2 9.0 %all_to_all.30 = bf16[4,32,128]{2,0,1:T(4,128)(2,1)S(1)} all-to-all(bf16[4,32,128]{2,0,1:T(4,128)(2,1)S(1)} %copy.24), channel_id=1, replica_groups=mesh['groups'=1,'row'=32] {'row'}, dimensions={1} | all-to-all | bytes 65536 | tf_op jit(solution)/shard_map/all_to_all | solution.py:117
  68.2 0.6 copy.50
  (26 shorter events, 0.3 us)
Async XLA Ops:
  0.0 58.4 %copy-start = (bf16[128,128]{1,0:T(8,128)(2,1)S(1)}, bf16[128,128]{1,0:T(8,128)(2,1)}, u32[]{:S(2)}) copy-start(bf16[128,128]{1,0:T(8,128)(2,1)} %param.20) | copy-start | bytes 98308
  0.0 1.8 %copy-start.1 = (bf16[4,128,128]{2,1,0:T(8,128)(2,1)S(1)}, bf16[4,128,128]{2,1,0:T(8,128)(2,1)}, u32[]{:S(2)}) copy-start(bf16[4,128,128]{2,1,0:T(8,128)(2,1)} %param.12) | copy-start | bytes 393220
  2.1 0.7 copy-start.3
  2.1 0.7 copy-start.4
  3.7 7.3 %copy-start.5 = (bf16[128,4]{0,1:T(4,128)(2,1)S(1)}, bf16[128,4]{0,1:T(4,128)(2,1)}, u32[]{:S(2)}) copy-start(bf16[128,4]{0,1:T(4,128)(2,1)} %param.18) | copy-start | bytes 3076
  3.7 50.4 %all-to-all-start = ((bf16[4,32,4,128]{3,0,2,1:T(4,128)(2,1)}), bf16[4,32,4,128]{3,0,2,1:T(4,128)(2,1)S(1)}, u32[]{:S(2)}, u32[]{:S(2)}) async-start(bf16[4,32,4,128]{3,0,2,1:T(4,128)(2,1)} %copy.18), calls=%async_computation | async-start | bytes 262144 | tf_op jit(solution)/shard_map/all_to_all | solution.py:115
  11.0 0.7 copy-start.6
  11.7 42.3 %copy-start.2 = (bf16[128,512]{1,0:T(8,128)(2,1)S(1)}, bf16[128,512]{1,0:T(8,128)(2,1)}, u32[]{:S(2)}) copy-start(bf16[128,512]{1,0:T(8,128)(2,1)} %param.17) | copy-start | bytes 393220
  58.3 0.7 copy-start.7
  58.4 0.7 copy-start.8
where the time goes:
time: 69 us; the launch traced here: 68.8 us
  blocking collectives  51.2 us (74%)
  starting transfers between devices  7.33 us (11%)
  local copies, waits for them, and re-layouts  4.59 us (7%)
  other arithmetic  2.97 us (4%)
  matrix products  2.33 us (3%)
    all_gather x1, blocking collectives, per_device(): key_bias = lax.all_gather(local_bias, 'row', axis=0, tiled=True)  42.2 us
    all_to_all x1, blocking collectives, per_device(): lax.all_to_all(result, 'row', split_axis=1, concat_axis=0, tiled=True)  8.95 us
    all_to_all x1, starting transfers between devices, per_device(): lax.all_to_all(split_pair, 'row', split_axis=1, concat_axis=0, tiled=True)  7.33 us
    unnamed x19, local copies, waits for them, and re-layouts  2.47 us
  transfers between devices with their start and end apart: 1, of which 0 were waited for; matrix products, arithmetic and copies ran while one was open for 0% of the time, Pallas kernels for 0%

commit v1 on v0

--- a/solution.py
+++ b/solution.py
@@ -112,7 +112,10 @@
     mask_bias = big_negative * (residue_mask.astype(jnp.float32) - 1.0)
     split_pair = normal.reshape(local_rows, devices_row, local_rows, channels)
     key_bias = lax.all_gather(local_bias, "row", axis=0, tiled=True)
-    received = lax.all_to_all(split_pair, "row", split_axis=1, concat_axis=0, tiled=True)
+    size = lax.axis_size("row")
+    blocks = jnp.stack(jnp.split(split_pair, size, axis=1), axis=0)
+    blocks = lax.all_to_all(blocks, "row", split_axis=0, concat_axis=0)
+    received = jnp.concatenate(blocks, axis=0)
     result = attend_whole(received[:, 0], key_bias, mask_bias, w_proj, gate_shift, w_out, out_shift)
     row_layout = lax.all_to_all(result, "row", split_axis=1, concat_axis=0, tiled=True)
     return jnp.transpose(row_layout, (1, 0, 2))

time: 69 us -> 87.4 us (1.27)
  local copies, waits for them, and re-layouts: 4.59 us -> 22.9 us
    unnamed x19 -> x50, local copies, waits for them, and re-layouts: 2.47 us -> 20.9 us
where the time goes in v1:
time: 87.4 us; the launch traced here: 87.1 us
  blocking collectives  51.2 us (59%)
  local copies, waits for them, and re-layouts  22.9 us (26%)
  starting transfers between devices  7.33 us (8%)
  other arithmetic  2.97 us (3%)
  matrix products  2.33 us (3%)
    all_gather x1, blocking collectives, per_device(): key_bias = lax.all_gather(local_bias, 'row', axis=0, tiled=True)  42.2 us
    unnamed x50, local copies, waits for them, and re-layouts  20.9 us
    all_to_all x1, blocking collectives, per_device(): lax.all_to_all(result, 'row', split_axis=1, concat_axis=0, tiled=True)  8.95 us
    all_to_all x1, starting transfers between devices, per_device(): blocks = lax.all_to_all(blocks, 'row', split_axis=0, concat_axis=0)  7.33 us
  transfers between devices with their start and end apart: 1, of which 0 were waited for; matrix products, arithmetic and copies ran while one was open for 0% of the time, Pallas kernels for 0%

profile of v1, /device:TPU:0, one launch (start us, length us, event | category | flops | bytes accessed | tf_op | source)
XLA Modules:
  0.0 87.1 jit_solution(5746787307515938993)
XLA Ops:
  0.0 0.7 fusion.32
  0.7 1.1 %fusion.12 = f32[4,128]{1,0:T(4,128)S(1)} fusion(bf16[4,128,128]{2,1,0:T(8,128)(2,1)} %param.12, f32[4,128]{1,0:T(4,128)S(1)} %bitcast.200), kind=kLoop, calls=%fused_computation.24 | loop fusion | flops 196096 | bytes 135168 | tf_op jit(solution)/shard_map/reduce_sum | solution.py:29
  1.8 0.2 multiply_reduce_fusion
  2.1 0.6 copy-done.3
  2.7 0.2 add_convert_fusion
  3.0 0.6 constant_dynamic-update-slice_fusion.32
  3.6 0.6 constant_dynamic-update-slice_fusion.31
  4.2 0.6 constant_dynamic-update-slice_fusion.30
  4.8 0.6 constant_dynamic-update-slice_fusion.29
  5.4 0.6 constant_dynamic-update-slice_fusion.28
  6.0 0.6 constant_dynamic-update-slice_fusion.27
  6.6 0.6 constant_dynamic-update-slice_fusion.26
  7.2 0.6 constant_dynamic-update-slice_fusion.25
  7.8 0.6 constant_dynamic-update-slice_fusion.24
  8.4 0.6 constant_dynamic-update-slice_fusion.23
  9.0 0.6 constant_dynamic-update-slice_fusion.22
  9.6 0.6 constant_dynamic-update-slice_fusion.21
  10.1 0.6 constant_dynamic-update-slice_fusion.20
  10.7 0.6 constant_dynamic-update-slice_fusion.19
  11.3 0.6 constant_dynamic-update-slice_fusion.18
  11.9 0.6 constant_dynamic-update-slice_fusion.17
  12.5 0.6 constant_dynamic-update-slice_fusion.16
  13.1 0.6 constant_dynamic-update-slice_fusion.15
  13.7 0.6 constant_dynamic-update-slice_fusion.14
  14.3 0.6 constant_dynamic-update-slice_fusion.13
  14.9 0.6 constant_dynamic-update-slice_fusion.12
  15.5 0.6 constant_dynamic-update-slice_fusion.11
  16.1 0.6 constant_dynamic-update-slice_fusion.10
  16.7 0.6 constant_dynamic-update-slice_fusion.9
  17.3 0.6 constant_dynamic-update-slice_fusion.8
  17.9 0.6 constant_dynamic-update-slice_fusion.7
  18.5 0.6 constant_dynamic-update-slice_fusion.6
  19.1 0.6 constant_dynamic-update-slice_fusion.5
  19.7 0.6 constant_dynamic-update-slice_fusion.4
  20.2 0.6 constant_dynamic-update-slice_fusion.3
  20.8 0.6 constant_dynamic-update-slice_fusion.2
  21.4 0.6 constant_dynamic-update-slice_fusion.1
  22.0 7.3 %all-to-all-start = ((bf16[32,4,1,4,128]{4,1,3,2,0:T(4,128)(2,1)}), bf16[32,4,1,4,128]{4,1,3,2,0:T(4,128)(2,1)S(1)}, u32[]{:S(2)}, u32[]{:S(2)}) async-start(bf16[32,4,1,4,128]{4,1,3,2,0:T(4,128)(2,1)} %constant_dynamic-update-slice_fusion.1), calls=%async_computation | async-start | bytes 262144 | tf_op jit(solution)/shard_map/all_to_all | solution.py:117
  29.4 0.1 fusion.10
  29.5 0.5 copy-done.6
  30.0 42.2 %all_gather.3 = bf16[128,4,32]{2,1,0:T(4,128)(2,1)S(1)} all-gather(bf16[4,4,32]{2,1,0:T(4,128)(2,1)S(1)} %fusion.10), channel_id=1, replica_groups=mesh['groups'=1,'row'=32] {'row'}, dimensions={0}, use_global_device_ids=true | all-gather | bytes 33792 | tf_op jit(solution)/shard_map/all_gather | solution.py:114
  72.5 0.2 fusion.8
  72.7 0.2 convolution_bitcast_fusion.2
  72.9 3.8 %while.10 = (s32[]{:T(128)}, f32[4,32,128]{2,1,0:T(8,128)S(1)}, bf16[4,128,256]{2,1,0:T(8,128)(2,1)S(1)}, bf16[4,32,128]{2,1,0:T(8,128)(2,1)S(1)}, bf16[128,4,32...) while((s32[]{:T(128)}, f32[4,32,128]{2,1,0:T(8,128)S(1)}, bf16[4,128,256]{2,1,0:T(8,128)(2,1)S(1)}, ...), condition=%wide.region_5.6_spmd, body=%wide.region_2.5_spmd.sunk | while | flops 2232066 | bytes 814169 | solution.py:88
  72.9 0.1 copy.259
  73.1 0.2 fusion.56
  73.4 0.2 fusion.57
  73.5 0.2 fusion.58
  73.9 0.1 copy.259
  74.1 0.2 fusion.56
  74.3 0.2 fusion.57
  74.5 0.2 fusion.58
  74.8 0.1 copy.259
  75.0 0.2 fusion.56
  75.3 0.2 fusion.57
  75.4 0.2 fusion.58
  75.7 0.1 copy.259
  76.0 0.2 fusion.56
  76.2 0.2 fusion.57
  76.4 0.2 fusion.58
  76.7 0.6 copy-done.7
  77.4 0.1 fusion.9
  77.5 9.0 %all_to_all.20 = bf16[4,32,128]{2,0,1:T(4,128)(2,1)S(1)} all-to-all(bf16[4,32,128]{2,0,1:T(4,128)(2,1)S(1)} %copy.117), channel_id=1, replica_groups=mesh['groups'=1,'row'=32] {'row'}, dimensions={1} | all-to-all | bytes 65536 | tf_op jit(solution)/shard_map/all_to_all | solution.py:120
  86.5 0.6 copy.302
  (53 shorter events, 1.1 us)
Async XLA Ops:
  0.0 76.7 %copy-start = (bf16[128,128]{1,0:T(8,128)(2,1)S(1)}, bf16[128,128]{1,0:T(8,128)(2,1)}, u32[]{:S(2)}) copy-start(bf16[128,128]{1,0:T(8,128)(2,1)} %param.20) | copy-start | bytes 98308
  0.0 1.8 %copy-start.1 = (bf16[4,128,128]{2,1,0:T(8,128)(2,1)S(1)}, bf16[4,128,128]{2,1,0:T(8,128)(2,1)}, u32[]{:S(2)}) copy-start(bf16[4,128,128]{2,1,0:T(8,128)(2,1)} %param.12) | copy-start | bytes 393220
  2.1 0.7 copy-start.3
  2.1 0.7 copy-start.4
  22.0 7.3 %copy-start.5 = (bf16[128,4]{0,1:T(4,128)(2,1)S(1)}, bf16[128,4]{0,1:T(4,128)(2,1)}, u32[]{:S(2)}) copy-start(bf16[128,4]{0,1:T(4,128)(2,1)} %param.18) | copy-start | bytes 3076
  22.0 50.4 %all-to-all-start = ((bf16[32,4,1,4,128]{4,1,3,2,0:T(4,128)(2,1)}), bf16[32,4,1,4,128]{4,1,3,2,0:T(4,128)(2,1)S(1)}, u32[]{:S(2)}, u32[]{:S(2)}) async-start(bf16[32,4,1,4,128]{4,1,3,2,0:T(4,128)(2,1)} %constant_dynamic-update-slice_fusion.1), calls=%async_computation | async-start | bytes 262144 | tf_op jit(solution)/shard_map/all_to_all | solution.py:117
  29.4 0.7 copy-start.6
  30.0 42.3 %copy-start.2 = (bf16[128,512]{1,0:T(8,128)(2,1)S(1)}, bf16[128,512]{1,0:T(8,128)(2,1)}, u32[]{:S(2)}) copy-start(bf16[128,512]{1,0:T(8,128)(2,1)} %param.17) | copy-start | bytes 393220
  76.7 0.7 copy-start.7
  76.7 0.7 copy-start.8
